TPU v7x, 256 devices: a whole 4x4x8 slice. The times are simulated.
256 devices in a mesh: row: 8 (over z_hi, y), col: 32 (over x, z_lo, core).
Axes of the slice: x: 4, y: 4, z: 8 (z_hi: 2, z_lo: 4; z = z_hi * 4 + z_lo), core: 2. Of those that a mesh axis runs over, the one named last changes fastest.
Arguments:
- query_latent: bfloat16 [1024, 73728], P('row', 'col'), may hold values from -48 to 48
- kv_latent: bfloat16 [6144, 576], P('col'), may hold values from -6 to 6
- index_query: bfloat16 [1024, 8192], P('row'), may hold values from -18 to 18
- index_key: bfloat16 [6144, 128], P('col'), may hold values from -6 to 6
- head_weight: float32 [1024, 64], P('row'), may hold values from 0.05 to 0.5
- chosen: int32 [1024, 96], P('row'), may hold values from 0 to 1, as said below
- loss_grad: float32 [1024], P('row'), may hold values from 200 to 2000
Outputs:
- grad_query: float32 [1024, 8192], P('row', 'col')
- grad_key: float32 [6144, 128], P('col')
- grad_weight: float32 [1024, 64], P('row', 'col')
Inputs may be any that keep to these rules, and one draw needn't show every extreme that they name: `chosen`: each query t has exactly 32 ones, all in blocks at or before the block that holds its position 5120 + t, and that block is always among them.
All inputs are finite; a program needn't handle non-finite values.
Results may differ from a plain program's by a relative error of at most 0.0033.
Values may be sent and summed in bfloat16 or wider, within the bound.
No kernel may reach another device: no remote copies, remote signals or barrier semaphores. Data moves between devices by JAX's collectives and lax.ppermute only.
A program may use at most 64 MiB of HBM per device.

v0:
```python
import jax
import jax.numpy as jnp
from jax import lax
from jax.sharding import PartitionSpec as P

mla_scale = 192.0 ** (-0.5)
big_negative = -1e30


def body(query_latent, kv_latent, index_query, index_key, head_weight, chosen, loss_grad):
    row_count = lax.axis_size("row")
    col_count = lax.axis_size("col")
    row_index = lax.axis_index("row")
    col_index = lax.axis_index("col")
    rows_local = query_latent.shape[0]
    keys_local = kv_latent.shape[0]
    latent = kv_latent.shape[1]
    all_keys = keys_local * col_count
    all_queries = rows_local * row_count
    heads_local = query_latent.shape[1] // latent
    total_heads = heads_local * col_count
    block_count = chosen.shape[1]
    block_len = all_keys // block_count
    index_dim = index_key.shape[1]
    index_heads = index_query.shape[1] // index_dim
    heads_mine = index_heads // col_count
    inverse = index_dim ** (-0.5)
    query_pos = lax.iota(jnp.int32, rows_local) + row_index * rows_local + (all_keys - all_queries)
    key_pos = lax.iota(jnp.int32, all_keys)
    expand = jnp.broadcast_to(chosen[:, :, None], (rows_local, block_count, block_len)).reshape(
        rows_local, all_keys
    )
    allowed = (key_pos[None, :] <= query_pos[:, None]) & (expand > 0)
    keys_all = lax.all_gather(kv_latent, "col", axis=0, tiled=True)
    queries = query_latent.reshape(rows_local, heads_local, latent)
    summed = jnp.zeros((rows_local, all_keys), jnp.float32)
    for head_index in range(heads_local):
        scores = (
            jnp.einsum(
                "td,sd->ts", queries[:, head_index, :], keys_all, preferred_element_type=jnp.float32
            )
            * mla_scale
        )
        masked = jnp.where(allowed, scores, big_negative)
        highest = jnp.max(masked, axis=1, keepdims=True)
        raised = jnp.where(allowed, jnp.exp(masked - highest), 0.0)
        summed = summed + raised / jnp.sum(raised, axis=1, keepdims=True)
    target = lax.psum_scatter(summed, "col", scatter_dimension=1, tiled=True) / total_heads
    local_allowed = lax.dynamic_slice_in_dim(allowed, col_index * keys_local, keys_local, 1)
    index_rows = index_query.reshape(rows_local, index_heads, index_dim)
    affinity = (
        jnp.einsum("tjd,sd->tjs", index_rows, index_key, preferred_element_type=jnp.float32)
        * inverse
    )
    logits = jnp.sum(head_weight[:, :, None] * jax.nn.softplus(affinity), axis=1)
    masked = jnp.where(local_allowed, logits, big_negative)
    highest = lax.pmax(jnp.max(masked, axis=1), "col")
    raised = jnp.where(local_allowed, jnp.exp(masked - highest[:, None]), 0.0)
    total = lax.psum(jnp.sum(raised, axis=1), "col")
    chance = raised / total[:, None]
    grad_logit = jnp.where(local_allowed, loss_grad[:, None] * (chance - target), 0.0).astype(
        jnp.bfloat16
    )
    grad_wide = lax.optimization_barrier(grad_logit).astype(jnp.float32)
    slopes = (grad_wide[:, None, :] * jax.nn.sigmoid(affinity)).astype(jnp.bfloat16)
    weighted = (head_weight[:, :, None] * index_rows).astype(jnp.bfloat16)
    key_part = jnp.einsum("tjs,tjd->sd", slopes, weighted, preferred_element_type=jnp.float32)
    grad_key = lax.psum(key_part, "row") * inverse
    own_start = col_index * heads_mine
    own_weight = lax.dynamic_slice_in_dim(head_weight, own_start, heads_mine, 1)
    query_part = jnp.einsum(
        "tjs,sd->tjd", slopes, index_key, preferred_element_type=jnp.float32
    ).reshape(rows_local, index_heads * index_dim)
    weight_part = jnp.sum(grad_wide[:, None, :] * jax.nn.softplus(affinity), axis=2)
    query_flat, grad_weight = (
        lax.psum_scatter(query_part, "col", scatter_dimension=1, tiled=True),
        lax.psum_scatter(weight_part, "col", scatter_dimension=1, tiled=True),
    )
    query_sum = query_flat.reshape(rows_local, heads_mine, index_dim)
    grad_query = (query_sum * (own_weight * inverse)[:, :, None]).reshape(
        rows_local, heads_mine * index_dim
    )
    return (grad_query, grad_key, grad_weight)


def solution(mesh):
    in_specs = (
        P("row", "col"),
        P("col", None),
        P("row", None),
        P("col", None),
        P("row", None),
        P("row", None),
        P("row"),
    )
    out_specs = (P("row", "col"), P("col", None), P("row", "col"))
    return jax.shard_map(body, mesh=mesh, in_specs=in_specs, out_specs=out_specs, check_vma=False)
```

profile of v0, /device:TPU:16, one launch (start us, length us, event | category | flops | bytes accessed | tf_op | source)
XLA Modules:
  0.0 522.7 jit_solution(10032148616950255443)
XLA Ops:
  7.2 0.0 copy-start
  7.2 0.0 all-gather.2.cloned.1.call-start
  7.2 0.7 all-gather.2.cloned.1.call-update
  7.9 0.0 reduce-scatter.7.cloned.1.call-start
  8.0 1.4 copy.32
  9.3 0.8 broadcast_compare_fusion
  10.2 0.6 fusion.4
  10.8 70.3 %all-gather.2.cloned.1.call-done = bf16[6144,576]{1,0:T(8,128)(2,1)} async-done(((bf16[192,576]{1,0:T(8,128)(2,1)}), bf16[6144,576]{1,0:T(8,128)(2,1)}) %all-gather.2.cloned.1.call-update) | async-done | bytes 7077904 | tf_op jit(solution)/shard_map/all_gather | solution.py:34
  81.1 0.0 copy-start.1
  81.1 5.2 fusion.26
  86.3 0.3 copy-done.1
  86.6 2.2 fusion.27
  88.8 2.2 fusion.28
  91.1 2.2 fusion.29
  93.3 2.6 fusion.5
  95.9 4.0 add_bitcast_fusion
  99.9 0.0 copy-start.3
  99.9 0.0 copy-start.5
  99.9 0.0 reduce-scatter.7.cloned.1.call-update
  99.9 0.2 all-reduce.3.cloned.1.call-start
  100.2 0.0 copy-done
  100.2 0.5 copy-done.3
  100.7 0.0 copy-done.5
  100.7 0.0 copy-start.4
  100.7 6.3 %multiply_reduce_fusion.1 = (f32[128,192]{0,1:T(8,128)S(1)}, f32[128,64,192]{0,2,1:T(8,128)}) fusion(f32[128,64]{0,1:T(8,128)S(1)} %copy-done.5, bf16[192,128]{1,0:T(8,128)(2,1)S(1)} %copy-done.3, bf16[128,8192]{1,0:T(8,128)(2,1)S(1)} %copy-done), kind=kOutput, calls=%fused_computation.11 | convolution fusion | flops 416784384 | bytes 8568832 | tf_op jit(solution)/shard_map/tjd,sd->tjs/dot_general | solution.py:52
  107.1 70.3 %pmax.7 = f32[128]{0:T(128)S(1)} all-reduce(f32[128]{0:T(128)S(1)} %fusion.22), channel_id=1, replica_groups=mesh['row'=8,'col'=32] {'col'}, use_global_device_ids=true, to_apply=%region_2.3 | all-reduce | flops 128 | bytes 1024 | tf_op jit(solution)/shard_map/pmax | solution.py:57
  177.4 0.1 fusion.21
  177.4 67.7 %psum.14 = f32[128]{0:T(128)S(1)} all-reduce(f32[128]{0:T(128)S(1)} %fusion.21), channel_id=1, replica_groups=mesh['row'=8,'col'=32] {'col'}, use_global_device_ids=true, to_apply=%region_4.5 | all-reduce | flops 128 | bytes 1024 | tf_op jit(solution)/shard_map/psum | solution.py:59
  245.2 5.3 %reduce-scatter.7.cloned.1.call-done = f32[192,128]{1,0:T(8,128)} async-done(((f32[6144,128]{1,0:T(8,128)}), f32[192,128]{1,0:T(8,128)}) %reduce-scatter.7.cloned.1.call-update) | async-done | bytes 98320
  250.4 0.0 copy-done.4
  250.4 0.9 fusion.20
  251.4 7.9 %multiply_reduce_fusion = (f32[128,64]{0,1:T(8,128)S(1)}, bf16[128,64,192]{0,2,1:T(8,128)(2,1)S(1)}) fusion(f32[128,192]{0,1:T(8,128)S(1)} %convert_element_type.16, f32[128,64,192]{0,2,1:T(8,128)} %get-tuple-element.18), kind=kLoop, calls=%fused_computation.9 | loop fusion | flops 22011904 | bytes 9568256 | tf_op jit(solution)/shard_map/reduce_sum | solution.py:74
  259.3 0.0 copy-start.2
  259.3 1.7 copy-done.2
  261.0 2.2 fusion.16
  263.2 0.0 all-reduce.3.cloned.1.call-update
  263.2 0.0 reduce-scatter.5.cloned.1.call-start
  263.2 4.6 fusion.23
  267.8 5.6 %copy.39 = f32[128,8192]{1,0:T(8,128)} copy(f32[128,8192]{0,1:T(8,128)} %bitcast.83) | data formatting | bytes 8388608 | tf_op jit(solution)/shard_map/reshape | solution.py:73
  273.5 0.0 copy-start.6
  273.5 0.0 reduce-scatter.5.cloned.1.call-update
  273.5 0.1 copy.40
  273.7 0.5 copy-done.6
  274.2 0.6 dynamic-slice
  275.4 134.5 %all-reduce = f32[128,64]{0,1:T(8,128)S(1)} all-reduce(f32[128,64]{0,1:T(8,128)S(1)} %get-tuple-element.7), channel_id=4, replica_groups=mesh['row'=8,'col'=32] {'col'}, use_global_device_ids=true, to_apply=%region_17.18.clone | all-reduce | flops 8192 | bytes 65536
  409.9 0.6 constant_dynamic-slice_fusion
  410.4 0.0 all-reduce.3.cloned.1.call-done
  410.4 1.5 broadcast_multiply_fusion
  412.0 102.4 %reduce-scatter.5.cloned.1.call-done = f32[128,256]{1,0:T(8,128)} async-done(((f32[128,8192]{1,0:T(8,128)}), f32[128,256]{1,0:T(8,128)}) %reduce-scatter.5.cloned.1.call-update) | async-done | bytes 131088 | tf_op jit(solution)/shard_map/reduce_scatter | solution.py:76
  514.4 0.2 mul.105
  514.6 1.6 bitcast_multiply_fusion
  (4 shorter events, 0.1 us)
Async XLA Ops:
  7.2 93.0 %copy-start = (bf16[128,8192]{1,0:T(8,128)(2,1)S(1)}, bf16[128,8192]{1,0:T(8,128)(2,1)}, u32[]{:S(2)}) copy-start(bf16[128,8192]{1,0:T(8,128)(2,1)} %param.9) | copy-start | bytes 6291460
  7.2 73.9 %all-gather.2.cloned.1.call-start = ((), (), s32[]{:S(2)}) async-start(), calls=%async_computation.2 | async-start | bytes 8110080 | tf_op jit(solution)/shard_map/all_gather | solution.py:34
  7.9 242.5 %reduce-scatter.7.cloned.1.call-start = ((), (), s32[]{:S(2)}) async-start(), calls=%async_computation.5 | async-start | bytes 3244032
  81.1 5.5 %copy-start.1 = (bf16[6144,576]{1,0:T(8,128)(2,1)S(1)}, bf16[6144,576]{1,0:T(8,128)(2,1)}, u32[]{:S(2)}) copy-start(bf16[6144,576]{1,0:T(8,128)(2,1)} %all-gather.2.cloned.1.call-done) | copy-start | bytes 21233668
  99.9 0.8 copy-start.3
  99.9 0.8 copy-start.5
  99.9 310.5 %all-reduce.3.cloned.1.call-start = ((), (), s32[]{:S(2)}) async-start(), calls=%async_computation.4 | async-start | bytes 196608 | tf_op jit(solution)/shard_map/psum | solution.py:68
  100.7 149.7 %copy-start.4 = (f32[128]{0:T(128)S(1)}, f32[128]{0:T(128)}, u32[]{:S(2)}) copy-start(f32[128]{0:T(128)} %param.13) | copy-start | bytes 1540
  259.3 1.7 copy-start.2
  263.2 251.2 %reduce-scatter.5.cloned.1.call-start = ((), (), s32[]{:S(2)}) async-start(), calls=%async_computation.3 | async-start | bytes 4325376 | tf_op jit(solution)/shard_map/reduce_scatter | solution.py:76
  273.5 0.7 copy-start.6
Sparse Core Ops, SparseCore 0:
  9.8 71.1 all-gather.1
  100.1 150.3 reduce-scatter.6
  263.3 92.9 all-reduce.2
  358.7 155.6 reduce-scatter.4
where the time goes:
time: 523 us
  blocking collectives  272 us (52%)
  waiting for transfers between devices  179 us (34%)
  matrix products  25.1 us (5%)
  other arithmetic  20.1 us (4%)
  between operations  14.5 us (3%)
  local copies, waits for them, and re-layouts  11.5 us (2%)
    unnamed x1, blocking collectives  134 us
    reduce_scatter x1, waiting for transfers between devices, body(): lax.psum_scatter(query_part, 'col', scatter_dimension=1, tiled=True)  102 us
    pmax x1, blocking collectives, body(): highest = lax.pmax(jnp.max(masked, axis=1), 'col')  70.3 us
    all_gather x1, waiting for transfers between devices, body(): keys_all = lax.all_gather(kv_latent, 'col', axis=0, tiled=True)  70.3 us
    psum x1, blocking collectives, body(): total = lax.psum(jnp.sum(raised, axis=1), 'col')  67.7 us
    dot_general x4, matrix products, body(): jnp.einsum('td,sd->ts', queries[:, head_index, :], keys_all, preferred_el...  11.9 us
  transfers between devices with their start and end apart: 4, of which 3 were waited for; matrix products, arithmetic and copies ran while one was open for 4% of the time, Pallas kernels for 0%

commit v1 on v0

--- a/solution.py
+++ b/solution.py
@@ -31,7 +31,9 @@
         rows_local, all_keys
     )
     allowed = (key_pos[None, :] <= query_pos[:, None]) & (expand > 0)
-    keys_all = lax.all_gather(kv_latent, "col", axis=0, tiled=True)
+    keys_all = jnp.concatenate(
+        lax.all_to_all(jnp.stack([kv_latent] * lax.axis_size("col")), "col", 0, 0), axis=0
+    )
     queries = query_latent.reshape(rows_local, heads_local, latent)
     summed = jnp.zeros((rows_local, all_keys), jnp.float32)
     for head_index in range(heads_local):

time: 523 us -> 644 us (1.23)
  waiting for transfers between devices: 179 us -> 283 us
  starting transfers between devices: 0.34 us -> 9.3 us
    all_to_all x0 -> x1, waiting for transfers between devices: none -> 173 us  [body(): lax.all_to_all(jnp.stack([kv_latent] * lax.axis_size('col')), 'col', 0, 0)]
    all_gather x1 -> x0, waiting for transfers between devices: 70.3 us -> none  [body(): keys_all = lax.all_gather(kv_latent, 'col', axis=0, tiled=True)]
    all_to_all x0 -> x1, starting transfers between devices: none -> 8.99 us  [body(): lax.all_to_all(jnp.stack([kv_latent] * lax.axis_size('col')), 'col', 0, 0)]
  transfers between devices with their start and end apart: 4 -> 4, of which waited for: 3 -> 3; matrix products, arithmetic and copies ran while one was open for 4% -> 3% of each run, Pallas kernels for 0% -> 0%
where the time goes in v1:
time: 644 us; the launch traced here: 643 us
  waiting for transfers between devices  283 us (44%)
  blocking collectives  270 us (42%)
  matrix products  31.3 us (5%)
  other arithmetic  19.3 us (3%)
  local copies, waits for them, and re-layouts  15.4 us (2%)
  between operations  14.6 us (2%)
  starting transfers between devices  9.3 us (1%)
    all_to_all x1, waiting for transfers between devices, body(): lax.all_to_all(jnp.stack([kv_latent] * lax.axis_size('col')), 'col', 0, 0)  173 us
    unnamed x1, blocking collectives  134 us
    reduce_scatter x1, waiting for transfers between devices, body(): lax.psum_scatter(query_part, 'col', scatter_dimension=1, tiled=True)  103 us
    psum x1, blocking collectives, body(): total = lax.psum(jnp.sum(raised, axis=1), 'col')  67.8 us
    pmax x1, blocking collectives, body(): highest = lax.pmax(jnp.max(masked, axis=1), 'col')  67.6 us
    dot_general x4, matrix products, body(): jnp.einsum('td,sd->ts', queries[:, head_index, :], keys_all, preferred_el...  18.1 us
  transfers between devices with their start and end apart: 4, of which 3 were waited for; matrix products, arithmetic and copies ran while one was open for 3% of the time, Pallas kernels for 0%

profile of v1, /device:TPU:16, one launch (start us, length us, event | category | flops | bytes accessed | tf_op | source)
XLA Modules:
  0.0 642.8 jit_solution(14419429402350960341)
XLA Ops:
  7.2 0.0 copy-start
  7.2 5.3 stack.2
  12.5 0.0 copy-start.2
  12.5 0.0 copy-start.4
  12.5 9.0 %all-to-all-start = ((bf16[32,192,576]{2,1,0:T(8,128)(2,1)}), bf16[32,192,576]{2,1,0:T(8,128)(2,1)}, u32[]{:S(2)}, u32[]{:S(2)}) async-start(bf16[32,192,576]{2,1,0:T(8,128)(2,1)} %stack.2), calls=%async_computation | async-start | bytes 15728640 | tf_op jit(solution)/shard_map/all_to_all | solution.py:35
  21.5 0.0 reduce-scatter.7.cloned.1.call-start
  21.6 0.0 copy-done.2
  21.6 0.3 copy.32
  21.9 0.0 copy-done.4
  21.9 0.6 fusion.4
  22.6 172.9 %all-to-all-done = bf16[32,192,576]{2,1,0:T(8,128)(2,1)} async-done(((bf16[32,192,576]{2,1,0:T(8,128)(2,1)}), bf16[32,192,576]{2,1,0:T(8,128)(2,1)}, u32[]{:S(2)}, u32[]{:S(2)}) %all-to-all-start) | async-done | bytes 7077920 | tf_op jit(solution)/shard_map/all_to_all | solution.py:35
  195.4 4.5 fusion.26
  200.0 4.5 fusion.27
  204.5 4.5 fusion.28
  209.1 4.5 fusion.29
  213.6 2.6 fusion.5
  216.2 4.0 add_bitcast_fusion
  220.2 0.0 copy-start.3
  220.2 0.0 copy-start.6
  220.2 0.0 reduce-scatter.7.cloned.1.call-update
  220.2 0.2 all-reduce.3.cloned.1.call-start
  220.5 0.0 copy-done
  220.5 0.5 copy-done.3
  221.0 0.0 copy-done.6
  221.0 0.0 copy-start.5
  221.0 6.3 multiply_reduce_fusion.1
  227.4 67.6 %pmax.7 = f32[128]{0:T(128)S(1)} all-reduce(f32[128]{0:T(128)S(1)} %fusion.22), channel_id=1, replica_groups=mesh['row'=8,'col'=32] {'col'}, use_global_device_ids=true, to_apply=%region_2.3 | all-reduce | flops 128 | bytes 1024 | tf_op jit(solution)/shard_map/pmax | solution.py:59
  295.0 0.1 fusion.21
  295.0 67.8 %psum.14 = f32[128]{0:T(128)S(1)} all-reduce(f32[128]{0:T(128)S(1)} %fusion.21), channel_id=1, replica_groups=mesh['row'=8,'col'=32] {'col'}, use_global_device_ids=true, to_apply=%region_4.5 | all-reduce | flops 128 | bytes 1024 | tf_op jit(solution)/shard_map/psum | solution.py:61
  362.8 7.0 %reduce-scatter.7.cloned.1.call-done = f32[192,128]{1,0:T(8,128)} async-done(((f32[6144,128]{1,0:T(8,128)}), f32[192,128]{1,0:T(8,128)}) %reduce-scatter.7.cloned.1.call-update) | async-done | bytes 98320
  369.9 0.0 copy-done.5
  369.9 0.9 fusion.20
  370.8 7.9 %multiply_reduce_fusion = (f32[128,64]{0,1:T(8,128)S(1)}, bf16[128,64,192]{0,2,1:T(8,128)(2,1)S(1)}) fusion(f32[128,192]{0,1:T(8,128)S(1)} %convert_element_type.16, f32[128,64,192]{0,2,1:T(8,128)} %get-tuple-element.18), kind=kLoop, calls=%fused_computation.9 | loop fusion | flops 22011904 | bytes 9568256 | tf_op jit(solution)/shard_map/reduce_sum | solution.py:76
  378.7 0.0 copy-start.1
  378.7 1.7 copy-done.1
  380.4 2.2 fusion.16
  382.6 0.0 all-reduce.3.cloned.1.call-update
  382.6 0.0 reduce-scatter.5.cloned.1.call-start
  382.7 4.6 fusion.23
  387.3 5.6 copy.39
  392.9 0.0 copy-start.7
  392.9 0.0 reduce-scatter.5.cloned.1.call-update
  393.0 0.1 copy.40
  393.1 0.5 copy-done.7
  393.6 0.6 dynamic-slice
  394.8 134.2 %all-reduce = f32[128,64]{0,1:T(8,128)S(1)} all-reduce(f32[128,64]{0,1:T(8,128)S(1)} %get-tuple-element.7), channel_id=4, replica_groups=mesh['row'=8,'col'=32] {'col'}, use_global_device_ids=true, to_apply=%region_17.18.clone | all-reduce | flops 8192 | bytes 65536
  529.0 0.6 constant_dynamic-slice_fusion
  529.6 0.0 all-reduce.3.cloned.1.call-done
  529.6 1.5 broadcast_multiply_fusion
  531.1 103.3 %reduce-scatter.5.cloned.1.call-done = f32[128,256]{1,0:T(8,128)} async-done(((f32[128,8192]{1,0:T(8,128)}), f32[128,256]{1,0:T(8,128)}) %reduce-scatter.5.cloned.1.call-update) | async-done | bytes 131088 | tf_op jit(solution)/shard_map/reduce_scatter | solution.py:78
  634.5 0.2 mul.105
  634.7 1.6 bitcast_multiply_fusion
  (5 shorter events, 0.1 us)
Async XLA Ops:
  7.2 213.3 %copy-start = (bf16[128,8192]{1,0:T(8,128)(2,1)S(1)}, bf16[128,8192]{1,0:T(8,128)(2,1)}, u32[]{:S(2)}) copy-start(bf16[128,8192]{1,0:T(8,128)(2,1)} %param.9) | copy-start | bytes 6291460
  12.5 9.1 %copy-start.2 = (bf16[128,2304]{1,0:T(8,128)(2,1)S(1)}, bf16[128,2304]{1,0:T(8,128)(2,1)}, u32[]{:S(2)}) copy-start(bf16[128,2304]{1,0:T(8,128)(2,1)} %param.7) | copy-start | bytes 1769476
  12.5 9.4 %copy-start.4 = (s32[128,96]{0,1:T(8,128)S(1)}, s32[128,96]{0,1:T(8,128)}, u32[]{:S(2)}) copy-start(s32[128,96]{0,1:T(8,128)} %param.12) | copy-start | bytes 147460
  12.5 182.9 %all-to-all-start = ((bf16[32,192,576]{2,1,0:T(8,128)(2,1)}), bf16[32,192,576]{2,1,0:T(8,128)(2,1)}, u32[]{:S(2)}, u32[]{:S(2)}) async-start(bf16[32,192,576]{2,1,0:T(8,128)(2,1)} %stack.2), calls=%async_computation | async-start | bytes 15728640 | tf_op jit(solution)/shard_map/all_to_all | solution.py:35
  21.5 348.4 %reduce-scatter.7.cloned.1.call-start = ((), (), s32[]{:S(2)}) async-start(), calls=%async_computation.5 | async-start | bytes 3244032
  220.2 0.8 copy-start.3
  220.2 0.8 copy-start.6
  220.2 309.3 %all-reduce.3.cloned.1.call-start = ((), (), s32[]{:S(2)}) async-start(), calls=%async_computation.4 | async-start | bytes 196608 | tf_op jit(solution)/shard_map/psum | solution.py:70
  221.0 148.9 %copy-start.5 = (f32[128]{0:T(128)S(1)}, f32[128]{0:T(128)}, u32[]{:S(2)}) copy-start(f32[128]{0:T(128)} %param.13) | copy-start | bytes 1540
  378.7 1.7 copy-start.1
  382.6 251.8 %reduce-scatter.5.cloned.1.call-start = ((), (), s32[]{:S(2)}) async-start(), calls=%async_computation.3 | async-start | bytes 4325376 | tf_op jit(solution)/shard_map/reduce_scatter | solution.py:78
  392.9 0.7 copy-start.7
Sparse Core Ops, SparseCore 0:
  220.4 149.4 reduce-scatter.6
  382.7 93.6 all-reduce.2
  479.0 155.4 reduce-scatter.4
